TPU v7x, 32 devices: a whole 2x2x4 slice. The times are simulated.
32 devices in a mesh: dp: 8 (over y, x, core), sp: 4 (over z).
Axes of the slice: x: 2, y: 2, z: 4, core: 2. Of those that a mesh axis runs over, the one named last changes fastest.
Arguments:
- inputs: bfloat16 [16, 2048, 768], P('dp', 'sp'), may hold values from -6 to 6
- out_grad: bfloat16 [16, 2048, 768], P('dp', 'sp'), may hold values from -6 to 6
- segment_ids: int32 [16, 2048], P('dp'), may hold values from 0 to 7, as said below
- positions: int32 [16, 2048], P('dp'), may hold values from 0 to 1023, as said below
- norm1_gain: bfloat16 [768], replicated, may hold values from 0.5 to 1.5
- norm1_bias: bfloat16 [768], replicated, may hold values from -1.75 to 1.75
- norm2_gain: bfloat16 [768], replicated, may hold values from 0.5 to 1.5
- norm2_bias: bfloat16 [768], replicated, may hold values from -1.75 to 1.75
- query_weight: bfloat16 [768, 768], replicated, may hold values from -0.21875 to 0.21875
- query_bias: bfloat16 [768], replicated, may hold values from -1.75 to 1.75
- key_weight: bfloat16 [768, 64], replicated, may hold values from -0.21875 to 0.21875
- key_bias: bfloat16 [16], replicated, may hold values from -1.75 to 1.75
- value_weight: bfloat16 [768, 64], replicated, may hold values from -0.21875 to 0.21875
- value_bias: bfloat16 [64], replicated, may hold values from -1.75 to 1.75
- output_weight: bfloat16 [768, 768], replicated, may hold values from -2.5 to 2.5
- output_bias: bfloat16 [768], replicated, may hold values from -1.75 to 1.75
- hidden_weight: bfloat16 [768, 3072], replicated, may hold values from -0.21875 to 0.21875
- hidden_bias: bfloat16 [3072], replicated, may hold values from -1.75 to 1.75
- down_weight: bfloat16 [3072, 768], replicated, may hold values from -0.109375 to 0.109375
- down_bias: bfloat16 [768], replicated, may hold values from -1.75 to 1.75
Outputs:
- layer_out: bfloat16 [16, 2048, 768], P('dp', 'sp')
- input_grad: float32 [16, 2048, 768], P('dp', 'sp')
- norm1_gain_grad: float32 [768], P('sp')
- norm1_bias_grad: float32 [768], P('sp')
- norm2_gain_grad: float32 [768], P('sp')
- norm2_bias_grad: float32 [768], P('sp')
- query_weight_grad: float32 [768, 768], P('sp')
- query_bias_grad: float32 [768], P('sp')
- key_weight_grad: float32 [768, 64], P('sp')
- key_bias_grad: float32 [16], P('sp')
- value_weight_grad: float32 [768, 64], P('sp')
- value_bias_grad: float32 [64], P('sp')
- output_weight_grad: float32 [768, 768], P('sp')
- output_bias_grad: float32 [768], P('sp')
- hidden_weight_grad: float32 [768, 3072], P('sp')
- hidden_bias_grad: float32 [3072], P('sp')
- down_weight_grad: float32 [3072, 768], P('sp')
- down_bias_grad: float32 [768], P('sp')
Inputs may be any that keep to these rules, and one draw needn't show every extreme that they name: `segment_ids`: document numbers of a row start at 0 and rise by one at each of its 7 boundaries, so every row holds exactly 8 documents; the first document of every row holds exactly 1024 tokens and each other document fewer. `positions`: each token's place counted from 0 at the first token of its document.
All inputs are finite; a program needn't handle non-finite values.
Results may differ from a plain program's by a relative error of at most 0.0085.
The roundings to bfloat16 on the way count: a program that leaves them out, or rounds other values in their place, can miss the bound.
Values may be sent and summed in bfloat16 or wider, within the bound.
No kernel may reach another device: no remote copies, remote signals or barrier semaphores. Data moves between devices by JAX's collectives and lax.ppermute only.
A program may use at most 256 MiB of HBM per device.

v0:
```python
import jax
import jax.numpy as jnp
from jax import lax
from jax.sharding import PartitionSpec as P

ROT = 16
EPSILON = 1e-05


def norm_forward(token_rows, gain_vec, offset):
    row_mean = jnp.mean(token_rows, -1, keepdims=True)
    centered = token_rows - row_mean
    inverse = lax.rsqrt(jnp.mean(centered * centered, -1, keepdims=True) + EPSILON)
    normed = centered * inverse
    return (normed * gain_vec + offset, normed, inverse)


def norm_backward(grad_out, normed, inverse, gain_vec):
    scaled = grad_out * gain_vec
    inner_sum = jnp.mean(scaled * normed, -1, keepdims=True)
    grad_in = inverse * (scaled - jnp.mean(scaled, -1, keepdims=True) - normed * inner_sum)
    return (grad_in, jnp.sum(grad_out * normed, 0), jnp.sum(grad_out, 0))


def rope_tables(places):
    half_rot = ROT // 2
    frequency = 10000.0 ** (-(jnp.arange(half_rot, dtype=jnp.float32) * 2.0) / ROT)
    angles = places.astype(jnp.float32)[:, None] * frequency[None, :]
    return (jnp.cos(angles), jnp.sin(angles))


def rotate(values_in, cosine, sine_tab):
    half_rot = ROT // 2
    first_part = values_in[..., :half_rot]
    second_part = values_in[..., half_rot:ROT]
    return jnp.concatenate(
        [
            first_part * cosine - second_part * sine_tab,
            second_part * cosine + first_part * sine_tab,
            values_in[..., ROT:],
        ],
        -1,
    )


def times_transposed(matrix_a, matrix_b):
    return lax.dot_general(
        matrix_a, matrix_b, (((1,), (1,)), ((), ())), preferred_element_type=jnp.float32
    )


def transposed_times(matrix_a, matrix_b):
    return lax.dot_general(
        matrix_a, matrix_b, (((0,), (0,)), ((), ())), preferred_element_type=jnp.float32
    )


def block_mask(seg_query, index_query, segments_all, block_start, block_end, key_end):
    key_index = jnp.arange(key_end, dtype=jnp.int32)
    same_doc = seg_query[block_start:block_end][:, None] == segments_all[None, :key_end]
    earlier = key_index[None, :] <= index_query[block_start:block_end][:, None]
    return (same_doc & earlier)[:, None, :]


def attend_forward(queries, keys_all, values_all, seg_query, index_query, segments_all):
    row_count = queries.shape[0]
    head_dim = keys_all.shape[1]
    heads_here = queries.shape[1] // head_dim
    full_len = keys_all.shape[0]
    block_rows = 512
    scale_factor = head_dim ** (-0.5)
    outputs, lse_list = ([], [])
    for block_start in range(0, row_count, block_rows):
        block_end = block_start + block_rows
        key_end = min(full_len, block_end)
        query_block = queries[block_start:block_end].reshape(block_rows, heads_here, head_dim)
        scores = (
            jnp.einsum(
                "qhd,kd->qhk", query_block, keys_all[:key_end], preferred_element_type=jnp.float32
            )
            * scale_factor
        )
        allowed = block_mask(seg_query, index_query, segments_all, block_start, block_end, key_end)
        masked = jnp.where(allowed, scores, -1e30)
        top_score = jnp.max(masked, -1, keepdims=True)
        exponent = jnp.exp(masked - top_score)
        total_weight = jnp.sum(exponent, -1, keepdims=True)
        weights_blk = (exponent / total_weight).astype(jnp.bfloat16)
        out_block = jnp.einsum(
            "qhk,kd->qhd", weights_blk, values_all[:key_end], preferred_element_type=jnp.float32
        )
        outputs.append(out_block.reshape(block_rows, heads_here * head_dim).astype(jnp.bfloat16))
        lse_list.append(top_score + jnp.log(total_weight))
    return (jnp.concatenate(outputs, 0), lse_list)


def attend_backward(
    queries, keys_all, values_all, grad_heads, lse_list, seg_query, index_query, segments_all
):
    row_count = queries.shape[0]
    head_dim = keys_all.shape[1]
    heads_here = queries.shape[1] // head_dim
    full_len = keys_all.shape[0]
    block_rows = 512
    scale_factor = head_dim ** (-0.5)
    grad_query_parts = []
    grad_kv = jnp.zeros((full_len, 2 * head_dim), jnp.float32)
    for block_number, block_start in enumerate(range(0, row_count, block_rows)):
        block_end = block_start + block_rows
        key_end = min(full_len, block_end)
        query_block = queries[block_start:block_end].reshape(block_rows, heads_here, head_dim)
        grad_block = grad_heads[block_start:block_end].reshape(block_rows, heads_here, head_dim)
        scores = (
            jnp.einsum(
                "qhd,kd->qhk", query_block, keys_all[:key_end], preferred_element_type=jnp.float32
            )
            * scale_factor
        )
        allowed = block_mask(seg_query, index_query, segments_all, block_start, block_end, key_end)
        masked = jnp.where(allowed, scores, -1e30)
        probs_f = jnp.exp(masked - lse_list[block_number])
        weights_blk = probs_f.astype(jnp.bfloat16)
        grad_weights = jnp.einsum(
            "qhd,kd->qhk", grad_block, values_all[:key_end], preferred_element_type=jnp.float32
        )
        row_inner = jnp.sum(probs_f * grad_weights, -1, keepdims=True)
        grad_scores = (probs_f * (grad_weights - row_inner)).astype(jnp.bfloat16)
        grad_query_block = (
            jnp.einsum(
                "qhk,kd->qhd", grad_scores, keys_all[:key_end], preferred_element_type=jnp.float32
            )
            * scale_factor
        )
        grad_key_part = (
            jnp.einsum("qhk,qhd->kd", grad_scores, query_block, preferred_element_type=jnp.float32)
            * scale_factor
        )
        grad_value_part = jnp.einsum(
            "qhk,qhd->kd", weights_blk, grad_block, preferred_element_type=jnp.float32
        )
        grad_kv = grad_kv.at[:key_end].add(jnp.concatenate([grad_key_part, grad_value_part], 1))
        grad_query_parts.append(grad_query_block.reshape(block_rows, heads_here * head_dim))
    return (jnp.concatenate(grad_query_parts, 0), grad_kv)


def gelu_exact(values_in):
    return jax.nn.gelu(values_in, approximate=False)


def one_row(
    token_in,
    grad_in_row,
    segments,
    places_full,
    norm1_gain,
    norm1_bias,
    norm2_gain,
    norm2_bias,
    query_weight,
    query_bias,
    key_weight,
    key_bias,
    value_weight,
    value_bias,
    output_weight,
    output_bias,
    hidden_weight,
    hidden_bias,
    down_weight,
    down_bias,
):
    sp_count = lax.axis_size("sp")
    local_len = token_in.shape[0]
    model_width = token_in.shape[1]
    head_dim = key_weight.shape[1]
    rot_dims = key_bias.shape[0]
    heads_all = model_width // head_dim
    full_len = local_len * sp_count
    start_row = lax.axis_index("sp") * local_len
    places_local = lax.dynamic_slice_in_dim(places_full, start_row, local_len)
    cos_local, sin_local = rope_tables(places_local)
    full_index = jnp.arange(full_len, dtype=jnp.int32)
    token_rows = token_in.astype(jnp.float32)
    norm_one, normed_one, inverse_one = norm_forward(
        token_rows, norm1_gain.astype(jnp.float32), norm1_bias.astype(jnp.float32)
    )
    attn_input = norm_one.astype(jnp.bfloat16)
    key_shift = jnp.concatenate(
        [key_bias.astype(jnp.float32), jnp.zeros((head_dim - rot_dims,), jnp.float32)]
    )
    query_pre = jnp.dot(
        attn_input, query_weight, preferred_element_type=jnp.float32
    ) + query_bias.astype(jnp.float32)
    key_pre = jnp.dot(attn_input, key_weight, preferred_element_type=jnp.float32) + key_shift
    value_pre = jnp.dot(
        attn_input, value_weight, preferred_element_type=jnp.float32
    ) + value_bias.astype(jnp.float32)
    query_rot = rotate(
        query_pre.reshape(local_len, heads_all, head_dim),
        cos_local[:, None, :],
        sin_local[:, None, :],
    )
    query_rot = query_rot.reshape(local_len, model_width).astype(jnp.bfloat16)
    key_rot = rotate(key_pre, cos_local, sin_local).astype(jnp.bfloat16)
    kv_local = jnp.concatenate([key_rot, value_pre.astype(jnp.bfloat16)], 1)
    kv_full = lax.all_gather(kv_local, "sp", axis=0, tiled=True)
    keys_all = kv_full[:, :head_dim]
    values_all = kv_full[:, head_dim:]
    queries = lax.all_to_all(query_rot, "sp", split_axis=1, concat_axis=0, tiled=True)
    heads_out, lse_list = attend_forward(
        queries, keys_all, values_all, segments, full_index, segments
    )
    attn_local = lax.all_to_all(heads_out, "sp", split_axis=0, concat_axis=1, tiled=True)
    attn_branch = jnp.dot(
        attn_local, output_weight, preferred_element_type=jnp.float32
    ) + output_bias.astype(jnp.float32)
    norm_two, normed_two, inverse_two = norm_forward(
        token_rows, norm2_gain.astype(jnp.float32), norm2_bias.astype(jnp.float32)
    )
    mlp_input = norm_two.astype(jnp.bfloat16)
    pre_act = jnp.dot(
        mlp_input, hidden_weight, preferred_element_type=jnp.float32
    ) + hidden_bias.astype(jnp.float32)
    activated, gelu_pull = jax.vjp(gelu_exact, pre_act)
    act_low = activated.astype(jnp.bfloat16)
    mlp_branch = jnp.dot(
        act_low, down_weight, preferred_element_type=jnp.float32
    ) + down_bias.astype(jnp.float32)
    layer_row = (token_rows + attn_branch + mlp_branch).astype(jnp.bfloat16)
    grad_rows_f = grad_in_row.astype(jnp.float32)
    grad_act = times_transposed(grad_in_row, down_weight)
    grad_pre_low = gelu_pull(grad_act)[0].astype(jnp.bfloat16)
    down_weight_grad = transposed_times(act_low, grad_in_row)
    down_bias_grad = jnp.sum(grad_rows_f, 0)
    hidden_weight_grad = transposed_times(mlp_input, grad_pre_low)
    hidden_bias_grad = jnp.sum(grad_pre_low.astype(jnp.float32), 0)
    grad_norm_two = times_transposed(grad_pre_low, hidden_weight)
    mlp_back, norm2_gain_grad, norm2_bias_grad = norm_backward(
        grad_norm_two, normed_two, inverse_two, norm2_gain.astype(jnp.float32)
    )
    grad_attn_low = times_transposed(grad_in_row, output_weight).astype(jnp.bfloat16)
    output_weight_grad = transposed_times(attn_local, grad_in_row)
    grad_heads = lax.all_to_all(grad_attn_low, "sp", split_axis=1, concat_axis=0, tiled=True)
    grad_queries, grad_kv = attend_backward(
        queries, keys_all, values_all, grad_heads, lse_list, segments, full_index, segments
    )
    cos_full, sin_full = rope_tables(places_full)
    heads_here = grad_queries.shape[1] // head_dim
    grad_query_full = rotate(
        grad_queries.reshape(full_len, heads_here, head_dim),
        cos_full[:, None, :],
        -sin_full[:, None, :],
    )
    grad_query_full = grad_query_full.reshape(full_len, heads_here * head_dim).astype(jnp.bfloat16)
    grad_query_local = lax.all_to_all(
        grad_query_full, "sp", split_axis=0, concat_axis=1, tiled=True
    )
    grad_kv_local = lax.psum_scatter(grad_kv, "sp", scatter_dimension=0, tiled=True)
    grad_key_low = rotate(grad_kv_local[:, :head_dim], cos_local, -sin_local).astype(jnp.bfloat16)
    grad_value_low = grad_kv_local[:, head_dim:].astype(jnp.bfloat16)
    query_weight_grad = transposed_times(attn_input, grad_query_local)
    query_bias_grad = jnp.sum(grad_query_local.astype(jnp.float32), 0)
    key_weight_grad = transposed_times(attn_input, grad_key_low)
    key_bias_grad = jnp.sum(grad_key_low[:, :rot_dims].astype(jnp.float32), 0)
    value_weight_grad = transposed_times(attn_input, grad_value_low)
    value_bias_grad = jnp.sum(grad_value_low.astype(jnp.float32), 0)
    grad_norm_one = (
        times_transposed(grad_query_local, query_weight)
        + times_transposed(grad_key_low, key_weight)
        + times_transposed(grad_value_low, value_weight)
    )
    attn_back, norm1_gain_grad, norm1_bias_grad = norm_backward(
        grad_norm_one, normed_one, inverse_one, norm1_gain.astype(jnp.float32)
    )
    input_row = grad_rows_f + attn_back + mlp_back
    grad_list = [
        norm1_gain_grad,
        norm1_bias_grad,
        norm2_gain_grad,
        norm2_bias_grad,
        query_weight_grad,
        query_bias_grad,
        key_weight_grad,
        key_bias_grad,
        value_weight_grad,
        value_bias_grad,
        output_weight_grad,
        down_bias_grad,
        hidden_weight_grad,
        hidden_bias_grad,
        down_weight_grad,
        down_bias_grad,
    ]
    return (layer_row, input_row, grad_list)


def on_device(
    inputs,
    out_grad,
    segment_ids,
    positions,
    norm1_gain,
    norm1_bias,
    norm2_gain,
    norm2_bias,
    query_weight,
    query_bias,
    key_weight,
    key_bias,
    value_weight,
    value_bias,
    output_weight,
    output_bias,
    hidden_weight,
    hidden_bias,
    down_weight,
    down_bias,
):
    sp_count = lax.axis_size("sp")
    params_all = (
        norm1_gain,
        norm1_bias,
        norm2_gain,
        norm2_bias,
        query_weight,
        query_bias,
        key_weight,
        key_bias,
        value_weight,
        value_bias,
        output_weight,
        output_bias,
        hidden_weight,
        hidden_bias,
        down_weight,
        down_bias,
    )
    layer_rows, input_rows = ([], [])
    grad_list = None
    for row_number in range(inputs.shape[0]):
        layer_row, input_row, row_grads = one_row(
            inputs[row_number],
            out_grad[row_number],
            segment_ids[row_number],
            positions[row_number],
            *params_all
        )
        layer_rows.append(layer_row)
        input_rows.append(input_row)
        if grad_list is None:
            grad_list = row_grads
        else:
            grad_list = [total + part for total, part in zip(grad_list, row_grads)]
    layer_out = jnp.stack(layer_rows, 0)
    input_grad = jnp.stack(input_rows, 0)
    flat_parts = [each_grad.reshape(sp_count, -1) for each_grad in grad_list]
    part_sizes = [piece.shape[1] for piece in flat_parts]
    packed = jnp.concatenate(flat_parts, 1)
    own_row = lax.psum_scatter(packed, "sp", scatter_dimension=0, tiled=True)
    summed = lax.psum(own_row, "dp").reshape(-1)
    results = []
    offset_now = 0
    for each_grad, size_now in zip(grad_list, part_sizes):
        shard_shape = (each_grad.shape[0] // sp_count,) + each_grad.shape[1:]
        results.append(summed[offset_now : offset_now + size_now].reshape(shard_shape))
        offset_now = offset_now + size_now
    return (layer_out, input_grad) + tuple(results)


def solution(mesh):
    placed = (
        P("dp", "sp", None),
        P("dp", "sp", None),
        P("dp", None),
        P("dp", None),
        P(),
        P(),
        P(),
        P(),
        P(),
        P(),
        P(),
        P(),
        P(),
        P(),
        P(),
        P(),
        P(),
        P(),
        P(),
        P(),
    )
    return jax.shard_map(
        on_device,
        mesh=mesh,
        in_specs=placed,
        out_specs=(
            P("dp", "sp", None),
            P("dp", "sp", None),
            P("sp"),
            P("sp"),
            P("sp"),
            P("sp"),
            P("sp", None),
            P("sp"),
            P("sp", None),
            P("sp"),
            P("sp", None),
            P("sp"),
            P("sp", None),
            P("sp"),
            P("sp", None),
            P("sp"),
            P("sp", None),
            P("sp"),
        ),
        check_vma=False,
    )
```

profile of v0, /device:TPU:0, one launch (start us, length us, event | category | flops | bytes accessed | tf_op | source)
XLA Modules:
  0.0 1696.9 jit_solution(9105256135938720582)
XLA Ops:
  10.8 6.3 all-to-all-start.4
  46.2 16.8 all_gather.7
  63.0 3.0 copy.98
  68.2 3.0 copy.101
  72.8 4.9 fusion.278
  77.7 34.7 %multiply_convert_fusion.7 = (bf16[512,3072]{1,0:T(8,128)(2,1)}, f32[512,3072]{1,0:T(8,128)}, bf16[512,3072]{1,0:T(8,128)(2,1)}, f32[512,3072]{1,0:T(8,128)}, f32[512,3072]{1,0:T(8,128)}) fusion(f32[3072]{0:T(1024)S(1)} %copy-done.121, f32[512,3072]{1,0:T(8,128)S(1)} %fusion.278, bf16[768,3072]{1,0:T(8,128)(2,1)S(1)} %bitcast.595, ...), kind=kOutput, calls=%fused_computation.66 | convolution fusion | flops 2625896448 | bytes 36986880 | tf_op jit(solution)/shard_map/dot_general | solution.py:221
  112.5 7.6 convert_reduce_fusion
  120.0 9.0 convert_reduce_fusion.1
  129.6 4.9 fusion.280
  134.6 5.6 convolution_add_fusion.1
  140.2 14.0 reshape.1321
  154.1 4.8 fusion.192
  158.9 5.4 convolution_add_fusion
  164.4 12.0 reshape.1322
  186.4 3.0 fusion.41
  190.6 6.2 fusion.307
  196.8 5.5 all-to-all-start
  202.3 27.9 %all_gather.6 = bf16[2048,128]{0,1:T(8,128)(2,1)S(1)} all-gather(bf16[512,128]{0,1:T(8,128)(2,1)S(1)} %pad_maximum_fusion.10), channel_id=1, replica_groups=mesh['dp'=8,'sp'=4] {'sp'}, dimensions={0}, use_global_device_ids=true | all-gather | bytes 655360 | tf_op jit(solution)/shard_map/all_gather | solution.py:206
  230.2 7.1 fusion.305
  240.3 4.0 all-to-all-start.2
  252.7 7.2 all-to-all-done.2
  259.9 4.6 all-to-all-start.6
  271.1 9.9 all-to-all-done.6
  328.4 4.6 multiply_reduce_fusion.3
  333.0 5.2 multiply_convert_fusion.3
  357.8 6.0 fusion.298
  363.8 6.4 fusion
  370.3 7.8 fusion.157
  378.5 3.0 fusion.64
  381.5 8.6 multiply_reduce_fusion.1
  390.1 9.4 multiply_convert_fusion.1
  404.3 5.9 multiply_reduce_fusion
  410.2 6.5 multiply_convert_fusion
  422.5 3.6 all-to-all-start.3
  438.3 8.3 all-to-all-done.3
  446.6 4.2 all-to-all-start.1
  455.0 3.0 convert_element_type.387
  460.2 4.1 fusion.161
  464.2 6.2 fusion.59
  470.6 6.7 all-to-all-done.1
  477.3 3.5 all-to-all-start.5
  482.8 3.0 convert_element_type.401
  490.3 7.5 fusion.67
  501.5 3.5 all-to-all-start.7
  512.5 4.2 reshape.1320
  516.7 3.6 fusion.181
  520.3 16.7 all-to-all-done.7
  537.0 4.4 convolution_add_fusion.3
  541.4 4.3 reshape.1317
  547.9 3.1 fusion.304
  551.0 3.2 fusion.306
  584.0 5.2 fusion.110
  589.3 3.8 convert_reduce_fusion.4
  610.2 13.7 dynamic-update-slice.32
  625.4 49.6 %dynamic-update-slice.34 = f32[4,1501268]{1,0:T(4,128)} dynamic-update-slice(f32[4,1501268]{1,0:T(4,128)} %dynamic-update-slice.33, f32[4,589824]{1,0:T(4,128)} %reshape.1321, s32[]{} %constant.345, s32[]{} %constant.357) | dynamic-update-slice | bytes 18874372
  676.5 49.2 %dynamic-update-slice.36 = f32[4,1501268]{1,0:T(4,128)} dynamic-update-slice(f32[4,1501268]{1,0:T(4,128)} %dynamic-update-slice.35, f32[4,589824]{1,0:T(4,128)} %reshape.1322, s32[]{} %constant.345, s32[]{} %constant.359) | dynamic-update-slice | bytes 18874372
  728.4 7.1 fusion.302
  735.5 788.8 %all-reduce.9.cloned.1.call-done = f32[4,1501268]{1,0:T(4,128)} async-done(((f32[4,1501268]{1,0:T(4,128)}), f32[4,1501268]{1,0:T(4,128)}) %all-reduce.9.cloned.1.call-update) | async-done | bytes 24020304
  1524.2 12.7 constant_dynamic-slice_fusion
  1536.9 6.0 fusion.303
  1551.1 86.1 %all-reduce.7.cloned.1.call-done = f32[1,1501268]{1,0:T(1,128)} async-done(((f32[1,1501268]{1,0:T(1,128)}), f32[1,1501268]{1,0:T(1,128)}) %all-reduce.7.cloned.1.call-update) | async-done | bytes 6005088 | tf_op jit(solution)/shard_map/psum | solution.py:360
  1640.0 27.6 %slice_reduce_fusion = (f32[589824]{0:T(1024)}, f32[589824]{0:T(1024)S(1)}) fusion(f32[1,1501268]{1,0:T(1,128)} %all-reduce.7.cloned.1.call-done), kind=kLoop, calls=%fused_computation.133 | loop fusion | bytes 9437184 | tf_op jit(solution)/shard_map/slice | solution.py:365
  1667.5 3.4 reshape.1328
  1670.9 8.6 slice_reduce_fusion.2
  (534 shorter events, 255.6 us)
Async XLA Ops:
  7.2 26.2 %copy-start = (bf16[768,768]{1,0:T(8,128)(2,1)S(1)}, bf16[768,768]{1,0:T(8,128)(2,1)}, u32[]{:S(2)}) copy-start(bf16[768,768]{1,0:T(8,128)(2,1)} %param.48) | copy-start | bytes 3538948
  7.2 12.8 copy-start.89
  9.6 17.9 %copy-start.9 = (bf16[2,512,768]{2,1,0:T(8,128)(2,1)S(1)}, bf16[2,512,768]{2,1,0:T(8,128)(2,1)}, u32[]{:S(2)}) copy-start(bf16[2,512,768]{2,1,0:T(8,128)(2,1)} %param.40) | copy-start | bytes 4718596
  10.8 186.0 %all-to-all-start.4 = ((bf16[512,4,192]{0,2,1:T(8,128)(2,1)}), bf16[512,4,192]{0,2,1:T(8,128)(2,1)}, u32[]{:S(2)}, u32[]{:S(2)}) async-start(bf16[512,4,192]{0,2,1:T(8,128)(2,1)} %bitcast.61), calls=%async_computation.4 | async-start | bytes 1572864 | tf_op jit(solution)/shard_map/all_to_all | solution.py:243
  27.9 101.8 %copy-start.85 = (f32[512]{0:T(512)}, f32[512]{0:T(512)S(1)}, u32[]{:S(2)}) copy-start(f32[512]{0:T(512)S(1)} %get-tuple-element.347) | copy-start | bytes 6148
  28.5 101.1 %copy-start.90 = (f32[512]{0:T(512)}, f32[512]{0:T(512)S(1)}, u32[]{:S(2)}) copy-start(f32[512]{0:T(512)S(1)} %add_rsqrt_fusion.1) | copy-start | bytes 6148
  37.3 97.3 %copy-start.71 = (f32[768]{0:T(1024)}, f32[768]{0:T(1024)S(1)}, u32[]{:S(2)}) copy-start(f32[768]{0:T(1024)S(1)} %convert_element_type.350) | copy-start | bytes 9220
  44.3 26.9 %copy-start.115 = (f32[1,512]{1,0:T(1,128)}, f32[1,512]{1,0:T(1,128)S(1)}, u32[]{:S(2)}) copy-start(f32[1,512]{1,0:T(1,128)S(1)} %get-tuple-element.348) | copy-start | bytes 6148
  44.3 26.9 %copy-start.117 = (f32[1,512]{1,0:T(1,128)}, f32[1,512]{1,0:T(1,128)S(1)}, u32[]{:S(2)}) copy-start(f32[1,512]{1,0:T(1,128)S(1)} %get-tuple-element.349) | copy-start | bytes 6148
  63.0 9.7 copy-start.99
  63.0 9.8 copy-start.103
  72.8 39.6 %slice-start.5 = ((s8[4718592]{0:T(1024)(128)(4,1)}), s8[4194304]{0:T(1024)(128)(4,1)S(1)}, s32[]{:S(2)}) async-start(s8[4718592]{0:T(1024)(128)(4,1)} %bitcast.596), calls=%async_computation.19 | async-start | bytes 8388608
  77.7 34.7 %copy-start.14 = (bf16[2,512,768]{2,1,0:T(8,128)(2,1)S(1)}, bf16[2,512,768]{2,1,0:T(8,128)(2,1)}, u32[]{:S(2)}) copy-start(bf16[2,512,768]{2,1,0:T(8,128)(2,1)} %param.41) | copy-start | bytes 4718596
  77.7 34.7 %slice-start.6 = ((s8[4718592]{0:T(1024)(128)(4,1)}), s8[524288]{0:T(1024)(128)(4,1)S(1)}, s32[]{:S(2)}) async-start(s8[4718592]{0:T(1024)(128)(4,1)} %bitcast.596), calls=%async_computation.20 | async-start | bytes 1048576
  140.2 14.0 copy-start.15
  164.4 14.4 copy-start.113
  164.4 14.4 copy-start.114
  164.4 14.4 copy-start.131
  164.4 15.7 copy-start.35
  176.5 9.9 copy-start.109
  176.5 9.9 copy-start.110
  176.6 9.9 copy-start.122
  176.6 9.9 copy-start.123
  176.6 9.9 copy-start.128
  180.1 9.3 copy-start.111
  180.1 9.3 copy-start.112
  180.1 9.3 copy-start.134
  180.1 10.5 copy-start.34
  196.8 42.6 %all-to-all-start = ((bf16[512,4,192]{0,2,1:T(8,128)(2,1)}), bf16[512,4,192]{0,2,1:T(8,128)(2,1)S(1)}, u32[]{:S(2)}, u32[]{:S(2)}) async-start(bf16[512,4,192]{0,2,1:T(8,128)(2,1)} %bitcast.4), calls=%async_computation | async-start | bytes 1572864 | tf_op jit(solution)/shard_map/all_to_all | solution.py:209
  237.2 9.1 copy-start.79
  240.3 19.7 %all-to-all-start.2 = ((bf16[512,4,192]{0,2,1:T(8,128)(2,1)}), bf16[512,4,192]{0,2,1:T(8,128)(2,1)S(1)}, u32[]{:S(2)}, u32[]{:S(2)}) async-start(bf16[512,4,192]{0,2,1:T(8,128)(2,1)} %bitcast.34), calls=%async_computation.2 | async-start | bytes 1572864 | tf_op jit(solution)/shard_map/all_to_all | solution.py:209
  250.3 15.8 copy-start.22
  250.3 15.8 copy-start.78
  259.9 21.1 %all-to-all-start.6 = ((bf16[512,4,192]{0,2,1:T(8,128)(2,1)}), bf16[512,4,192]{0,2,1:T(8,128)(2,1)}, u32[]{:S(2)}, u32[]{:S(2)}) async-start(bf16[512,4,192]{0,2,1:T(8,128)(2,1)} %bitcast.80), calls=%async_computation.7 | async-start | bytes 1572864 | tf_op jit(solution)/shard_map/all_to_all | solution.py:243
  267.2 18.8 %copy-start.94 = (f32[512,3]{0,1:T(4,128)}, f32[512,3]{0,1:T(4,128)S(1)}, u32[]{:S(2)}) copy-start(f32[512,3]{0,1:T(4,128)S(1)} %log_add_fusion.3) | copy-start | bytes 18436
  283.2 24.8 %copy-start.40 = (bf16[1,512,192]{1,2,0:T(8,128)(2,1)}, bf16[1,512,192]{1,2,0:T(8,128)(2,1)S(1)}, u32[]{:S(2)}) copy-start(bf16[1,512,192]{1,2,0:T(8,128)(2,1)S(1)} %get-tuple-element.249) | copy-start | bytes 589828
  290.7 18.8 %copy-start.3 = (f32[512,3,1024]{2,0,1:T(8,128)}, f32[512,3,1024]{2,0,1:T(8,128)S(1)}, u32[]{:S(2)}) copy-start(f32[512,3,1024]{2,0,1:T(8,128)S(1)} %get-tuple-element.314) | copy-start | bytes 18874372
  292.3 17.3 %copy-start.92 = (f32[512,3]{0,1:T(4,128)}, f32[512,3]{0,1:T(4,128)S(1)}, u32[]{:S(2)}) copy-start(f32[512,3]{0,1:T(4,128)S(1)} %log_add_fusion.2) | copy-start | bytes 18436
  316.2 27.9 %copy-start.2 = (f32[512,3,1536]{2,0,1:T(8,128)}, f32[512,3,1536]{2,0,1:T(8,128)S(1)}, u32[]{:S(2)}) copy-start(f32[512,3,1536]{2,0,1:T(8,128)S(1)} %get-tuple-element.312) | copy-start | bytes 28311556
  353.1 57.2 %copy-start.1 = (f32[512,3,2048]{2,0,1:T(8,128)}, f32[512,3,2048]{2,0,1:T(8,128)S(1)}, u32[]{:S(2)}) copy-start(f32[512,3,2048]{2,0,1:T(8,128)S(1)} %get-tuple-element.310) | copy-start | bytes 37748740
  370.2 7.8 slice-start
  370.2 8.3 slice-start.2
  370.3 8.3 copy-start.27
  422.5 24.0 %all-to-all-start.3 = ((bf16[4,512,192]{1,2,0:T(8,128)(2,1)}), bf16[4,512,192]{1,2,0:T(8,128)(2,1)S(1)}, u32[]{:S(2)}, u32[]{:S(2)}) async-start(bf16[4,512,192]{1,2,0:T(8,128)(2,1)} %bitcast.510), calls=%async_computation.3 | async-start | bytes 1572864 | tf_op jit(solution)/shard_map/all_to_all | solution.py:213
  426.2 128.1 %reduce-scatter.3.cloned.1.call-start = ((), (), s32[]{:S(2)}) async-start(), calls=%async_computation.10 | async-start | bytes 1310720 | tf_op jit(solution)/shard_map/reduce_scatter | solution.py:258
  437.5 22.6 %copy-start.93 = (f32[512,3]{0,1:T(4,128)S(1)}, f32[512,3]{0,1:T(4,128)}, u32[]{:S(2)}) copy-start(f32[512,3]{0,1:T(4,128)} %copy-done.92) | copy-start | bytes 18436
  446.6 17.7 %copy-start.28 = (bf16[4,512,192]{1,2,0:T(8,128)(2,1)}, bf16[4,512,192]{1,2,0:T(8,128)(2,1)S(1)}, u32[]{:S(2)}) copy-start(bf16[4,512,192]{1,2,0:T(8,128)(2,1)S(1)} %all-to-all-done.3) | copy-start | bytes 2359300
  446.6 30.7 %all-to-all-start.1 = ((bf16[4,512,192]{1,2,0:T(8,128)(2,1)}), bf16[4,512,192]{1,2,0:T(8,128)(2,1)}, u32[]{:S(2)}, u32[]{:S(2)}) async-start(bf16[4,512,192]{1,2,0:T(8,128)(2,1)} %bitcast.526), calls=%async_computation.1 | async-start | bytes 1572864 | tf_op jit(solution)/shard_map/all_to_all | solution.py:213
  477.3 23.3 %all-to-all-start.5 = ((bf16[4,512,192]{1,2,0:T(8,128)(2,1)}), bf16[4,512,192]{1,2,0:T(8,128)(2,1)S(1)}, u32[]{:S(2)}, u32[]{:S(2)}) async-start(bf16[4,512,192]{1,2,0:T(8,128)(2,1)} %copy.106), calls=%async_computation.5 | async-start | bytes 1572864 | tf_op jit(solution)/shard_map/all_to_all | solution.py:255
  497.7 10.4 copy-start.16
  501.5 35.5 %all-to-all-start.7 = ((bf16[4,512,192]{1,2,0:T(8,128)(2,1)}), bf16[4,512,192]{1,2,0:T(8,128)(2,1)S(1)}, u32[]{:S(2)}, u32[]{:S(2)}) async-start(bf16[4,512,192]{1,2,0:T(8,128)(2,1)} %copy.111), calls=%async_computation.8 | async-start | bytes 1572864 | tf_op jit(solution)/shard_map/all_to_all | solution.py:255
  505.0 53.6 %reduce-scatter.5.cloned.1.call-start = ((), (), s32[]{:S(2)}) async-start(), calls=%async_computation.11 | async-start | bytes 1310720 | tf_op jit(solution)/shard_map/reduce_scatter | solution.py:258
  507.7 1016.6 %all-reduce.9.cloned.1.call-start = ((), (), s32[]{:S(2)}) async-start(), calls=%async_computation.13 | async-start | bytes 48041984
  512.5 24.5 %copy-start.100 = (f32[512]{0:T(512)S(1)}, f32[512]{0:T(512)}, u32[]{:S(2)}) copy-start(f32[512]{0:T(512)} %copy-done.98) | copy-start | bytes 6148
  537.0 10.1 copy-start.20
  547.9 12.4 copy-start.116
  551.0 15.5 copy-start.12
  558.6 9.9 copy-start.139
  593.1 8.7 copy-start.120
  593.1 10.0 copy-start.68
  593.1 12.1 copy-start.133
  593.1 15.7 copy-start.132
  625.4 49.6 %copy-start.105 = (f32[4,768]{1,0:T(4,128)S(1)}, f32[4,768]{1,0:T(4,128)}, u32[]{:S(2)}) copy-start(f32[4,768]{1,0:T(4,128)} %add.500) | copy-start | bytes 36868
  727.2 910.0 %all-reduce.7.cloned.1.call-start = ((), (), s32[]{:S(2)}) async-start(), calls=%async_computation.12 | async-start | bytes 12010496 | tf_op jit(solution)/shard_map/psum | solution.py:360
  (98 other events, 409.8 us)
Sparse Core Ops, SparseCore 0:
  432.3 37.6 reduce-scatter.2
  508.2 33.9 reduce-scatter.4
  727.3 796.9 all-reduce.8
  1537.0 100.1 all-reduce.6
where the time goes:
time: 1710 us; the launch traced here: 1700 us
  waiting for transfers between devices  927 us (54%)
  local copies, waits for them, and re-layouts  289 us (17%)
  matrix products  281 us (16%)
  other arithmetic  104 us (6%)
  blocking collectives  44.7 us (3%)
  starting transfers between devices  35.8 us (2%)
    unnamed x5, waiting for transfers between devices  789 us
    unnamed x319, local copies, waits for them, and re-layouts  155 us
    psum x1, waiting for transfers between devices, on_device(): summed = lax.psum(own_row, 'dp').reshape(-1)  86.1 us
    dot_general x12, matrix products, times_transposed(): lax.dot_general(matrix_a, matrix_b, (((1,), (1,)), ((), ())), preferred_e...  53.4 us
    all_gather x2, blocking collectives, one_row(): kv_full = lax.all_gather(kv_local, 'sp', axis=0, tiled=True)  44.7 us
    slice x7, local copies, waits for them, and re-layouts, on_device(): summed[offset_now:offset_now + size_now].reshape(shard_shape)  42.4 us
    dot_general x12, matrix products, transposed_times(): lax.dot_general(matrix_a, matrix_b, (((0,), (0,)), ((), ())), preferred_e...  41 us
    dot_general x2, matrix products, one_row(): jnp.dot(mlp_input, hidden_weight, preferred_element_type=jnp.float32)  39.5 us
  transfers between devices with their start and end apart: 12, of which 8 were waited for; matrix products, arithmetic and copies ran while one was open for 17% of the time, Pallas kernels for 0%

commit v1 on v0

--- a/solution.py
+++ b/solution.py
@@ -203,7 +203,8 @@
     query_rot = query_rot.reshape(local_len, model_width).astype(jnp.bfloat16)
     key_rot = rotate(key_pre, cos_local, sin_local).astype(jnp.bfloat16)
     kv_local = jnp.concatenate([key_rot, value_pre.astype(jnp.bfloat16)], 1)
-    kv_full = lax.all_gather(kv_local, "sp", axis=0, tiled=True)
+    repeated = jnp.stack([kv_local] * lax.axis_size("sp"))
+    kv_full = jnp.concatenate(lax.all_to_all(repeated, "sp", 0, 0), axis=0)
     keys_all = kv_full[:, :head_dim]
     values_all = kv_full[:, head_dim:]
     queries = lax.all_to_all(query_rot, "sp", split_axis=1, concat_axis=0, tiled=True)

time: 1710 us -> 1720 us (level)
  blocking collectives: 44.7 us -> 0 us
  waiting for transfers between devices: 927 us -> 962 us
    all_gather x2 -> x0, blocking collectives: 44.7 us -> none  [one_row(): kv_full = lax.all_gather(kv_local, 'sp', axis=0, tiled=True)]
    unnamed x319 -> x323, local copies, waits for them, and re-layouts: 155 us -> 156 us
  transfers between devices with their start and end apart: 12 -> 14, of which waited for: 8 -> 10; matrix products, arithmetic and copies ran while one was open for 17% -> 17% of each run, Pallas kernels for 0% -> 0%
where the time goes in v1:
time: 1720 us; the launch traced here: 1710 us
  waiting for transfers between devices  962 us (56%)
  local copies, waits for them, and re-layouts  297 us (17%)
  matrix products  284 us (17%)
  other arithmetic  107 us (6%)
  starting transfers between devices  45.6 us (3%)
    unnamed x5, waiting for transfers between devices  789 us
    unnamed x323, local copies, waits for them, and re-layouts  156 us
    psum x1, waiting for transfers between devices, on_device(): summed = lax.psum(own_row, 'dp').reshape(-1)  86.1 us
    dot_general x12, matrix products, times_transposed(): lax.dot_general(matrix_a, matrix_b, (((1,), (1,)), ((), ())), preferred_e...  56 us
    slice x7, local copies, waits for them, and re-layouts, on_device(): summed[offset_now:offset_now + size_now].reshape(shard_shape)  42.6 us
    dot_general x12, matrix products, transposed_times(): lax.dot_general(matrix_a, matrix_b, (((0,), (0,)), ((), ())), preferred_e...  41 us
    dot_general x2, matrix products, one_row(): jnp.dot(mlp_input, hidden_weight, preferred_element_type=jnp.float32)  39.6 us
    reshape x6, local copies, waits for them, and re-layouts, on_device(): flat_parts = [each_grad.reshape(sp_count, -1) for each_grad in grad_list]  35.6 us
  transfers between devices with their start and end apart: 14, of which 10 were waited for; matrix products, arithmetic and copies ran while one was open for 17% of the time, Pallas kernels for 0%

profile of v1, /device:TPU:0, one launch (start us, length us, event | category | flops | bytes accessed | tf_op | source)
XLA Modules:
  0.0 1712.0 jit_solution(8673797088254919025)
XLA Ops:
  25.6 6.5 all-to-all-start.4
  39.5 3.2 convolution_convert_fusion
  42.7 3.2 convolution_convert_fusion.1
  59.0 3.0 copy.98
  64.2 3.0 copy.102
  68.7 4.8 fusion.278
  73.7 34.7 %multiply_convert_fusion.7 = (bf16[512,3072]{1,0:T(8,128)(2,1)}, f32[512,3072]{1,0:T(8,128)}, bf16[512,3072]{1,0:T(8,128)(2,1)}, f32[512,3072]{1,0:T(8,128)}, f32[512,3072]{1,0:T(8,128)}) fusion(f32[3072]{0:T(1024)S(1)} %convert_element_type.353, f32[512,3072]{1,0:T(8,128)S(1)} %fusion.278, bf16[768,3072]{1,0:T(8,128)(2,1)S(1)} %bitcast.632, ...), kind=kOutput, calls=%fused_computation.66 | convolution fusion | flops 2625896448 | bytes 36986880 | tf_op jit(solution)/shard_map/dot_general | solution.py:222
  108.4 7.6 convert_reduce_fusion
  116.0 9.0 convert_reduce_fusion.1
  125.5 4.9 fusion.280
  130.5 5.6 convolution_add_fusion.1
  136.1 14.0 reshape.1333
  150.1 4.8 fusion.192
  154.9 5.4 convolution_add_fusion
  160.5 12.1 reshape.1334
  181.1 5.1 all-to-all-start.1
  190.1 10.0 all-to-all-done.1
  200.1 3.5 all-to-all-start.6
  204.8 7.1 fusion.307
  211.9 11.3 all-to-all-done.6
  223.1 4.4 all-to-all-start
  228.9 7.1 fusion.305
  238.0 9.2 all-to-all-done
  247.2 3.5 all-to-all-start.3
  260.1 10.2 all-to-all-done.3
  270.3 4.6 all-to-all-start.8
  281.4 13.1 all-to-all-done.8
  341.9 4.6 multiply_reduce_fusion.3
  346.4 5.2 multiply_convert_fusion.3
  371.3 6.0 fusion.298
  377.3 6.4 fusion
  383.7 7.8 fusion.157
  395.0 8.5 multiply_reduce_fusion.1
  403.5 9.4 multiply_convert_fusion.1
  417.7 5.9 multiply_reduce_fusion
  423.6 6.5 multiply_convert_fusion
  436.0 3.6 all-to-all-start.5
  451.7 17.9 %all-to-all-done.5 = bf16[4,512,192]{1,2,0:T(8,128)(2,1)S(1)} async-done(((bf16[4,512,192]{1,2,0:T(8,128)(2,1)}), bf16[4,512,192]{1,2,0:T(8,128)(2,1)S(1)}, u32[]{:S(2)}, u32[]{:S(2)}) %all-to-all-start.5) | async-done | bytes 786464 | tf_op jit(solution)/shard_map/all_to_all | solution.py:214
  469.6 4.2 all-to-all-start.2
  483.2 4.1 fusion.161
  487.2 6.1 fusion.59
  493.5 5.1 all-to-all-start.7
  508.0 7.5 fusion.67
  516.8 4.7 all-to-all-start.9
  528.9 4.2 reshape.1332
  533.2 3.6 fusion.181
  536.8 14.6 all-to-all-done.9
  551.4 4.5 convolution_add_fusion.3
  555.8 4.2 reshape.1329
  562.3 3.1 fusion.304
  565.4 3.2 fusion.306
  598.3 5.2 fusion.110
  603.6 3.8 convert_reduce_fusion.4
  624.6 13.8 dynamic-update-slice.32
  639.8 49.6 %dynamic-update-slice.34 = f32[4,1501268]{1,0:T(4,128)} dynamic-update-slice(f32[4,1501268]{1,0:T(4,128)} %dynamic-update-slice.33, f32[4,589824]{1,0:T(4,128)} %reshape.1333, s32[]{} %constant.345, s32[]{} %constant.357) | dynamic-update-slice | bytes 18874372
  690.9 49.3 %dynamic-update-slice.36 = f32[4,1501268]{1,0:T(4,128)} dynamic-update-slice(f32[4,1501268]{1,0:T(4,128)} %dynamic-update-slice.35, f32[4,589824]{1,0:T(4,128)} %reshape.1334, s32[]{} %constant.345, s32[]{} %constant.359) | dynamic-update-slice | bytes 18874372
  742.9 7.1 fusion.302
  749.9 789.2 %all-reduce.9.cloned.1.call-done = f32[4,1501268]{1,0:T(4,128)} async-done(((f32[4,1501268]{1,0:T(4,128)}), f32[4,1501268]{1,0:T(4,128)}) %all-reduce.9.cloned.1.call-update) | async-done | bytes 24020304
  1539.1 12.7 constant_dynamic-slice_fusion
  1551.9 6.0 fusion.303
  1566.0 86.1 %all-reduce.7.cloned.1.call-done = f32[1,1501268]{1,0:T(1,128)} async-done(((f32[1,1501268]{1,0:T(1,128)}), f32[1,1501268]{1,0:T(1,128)}) %all-reduce.7.cloned.1.call-update) | async-done | bytes 6005088 | tf_op jit(solution)/shard_map/psum | solution.py:361
  1654.9 27.6 %slice_reduce_fusion = (f32[589824]{0:T(1024)}, f32[589824]{0:T(1024)S(1)}) fusion(f32[1,1501268]{1,0:T(1,128)} %all-reduce.7.cloned.1.call-done), kind=kLoop, calls=%fused_computation.133 | loop fusion | bytes 9437184 | tf_op jit(solution)/shard_map/slice | solution.py:366
  1682.4 3.4 reshape.1340
  1685.8 8.6 slice_reduce_fusion.2
  (544 shorter events, 272.2 us)
Async XLA Ops:
  7.2 41.2 %copy-start = (bf16[768,768]{1,0:T(8,128)(2,1)S(1)}, bf16[768,768]{1,0:T(8,128)(2,1)}, u32[]{:S(2)}) copy-start(bf16[768,768]{1,0:T(8,128)(2,1)} %param.48) | copy-start | bytes 3538948
  12.7 112.8 %copy-start.85 = (f32[512]{0:T(512)}, f32[512]{0:T(512)S(1)}, u32[]{:S(2)}) copy-start(f32[512]{0:T(512)S(1)} %get-tuple-element.347) | copy-start | bytes 6148
  12.7 117.8 %copy-start.98 = (f32[512]{0:T(512)}, f32[512]{0:T(512)S(1)}, u32[]{:S(2)}) copy-start(f32[512]{0:T(512)S(1)} %get-tuple-element.346) | copy-start | bytes 6148
  14.7 110.8 %copy-start.90 = (f32[512]{0:T(512)}, f32[512]{0:T(512)S(1)}, u32[]{:S(2)}) copy-start(f32[512]{0:T(512)S(1)} %add_rsqrt_fusion.1) | copy-start | bytes 6148
  14.7 115.8 %copy-start.101 = (f32[512]{0:T(512)}, f32[512]{0:T(512)S(1)}, u32[]{:S(2)}) copy-start(f32[512]{0:T(512)S(1)} %add_rsqrt_fusion) | copy-start | bytes 6148
  16.8 33.6 %copy-start.11 = (bf16[512,768]{1,0:T(8,128)(2,1)}, bf16[512,768]{1,0:T(8,128)(2,1)S(1)}, u32[]{:S(2)}) copy-start(bf16[512,768]{1,0:T(8,128)(2,1)S(1)} %get-tuple-element.240) | copy-start | bytes 2359300
  25.6 154.6 %all-to-all-start.4 = ((bf16[4,512,128]{1,2,0:T(8,128)(2,1)}), bf16[4,512,128]{1,2,0:T(8,128)(2,1)}, u32[]{:S(2)}, u32[]{:S(2)}) async-start(bf16[4,512,128]{1,2,0:T(8,128)(2,1)} %stack.34), calls=%async_computation.4 | async-start | bytes 1048576 | tf_op jit(solution)/shard_map/all_to_all | solution.py:207
  32.1 13.8 copy-start.14
  32.1 13.8 copy-start.60
  32.1 13.8 copy-start.137
  53.0 77.5 %copy-start.71 = (f32[768]{0:T(1024)}, f32[768]{0:T(1024)S(1)}, u32[]{:S(2)}) copy-start(f32[768]{0:T(1024)S(1)} %convert_element_type.350) | copy-start | bytes 9220
  68.7 39.6 %slice-start.5 = ((s8[4718592]{0:T(1024)(128)(4,1)}), s8[4194304]{0:T(1024)(128)(4,1)S(1)}, s32[]{:S(2)}) async-start(s8[4718592]{0:T(1024)(128)(4,1)} %bitcast.633), calls=%async_computation.21 | async-start | bytes 8388608
  73.6 34.8 %copy-start.15 = (bf16[2,512,768]{2,1,0:T(8,128)(2,1)S(1)}, bf16[2,512,768]{2,1,0:T(8,128)(2,1)}, u32[]{:S(2)}) copy-start(bf16[2,512,768]{2,1,0:T(8,128)(2,1)} %param.41) | copy-start | bytes 4718596
  73.6 34.7 %slice-start.6 = ((s8[4718592]{0:T(1024)(128)(4,1)}), s8[524288]{0:T(1024)(128)(4,1)S(1)}, s32[]{:S(2)}) async-start(s8[4718592]{0:T(1024)(128)(4,1)} %bitcast.633), calls=%async_computation.22 | async-start | bytes 1048576
  136.1 14.0 copy-start.16
  160.4 14.3 copy-start.80
  160.4 14.3 copy-start.89
  160.4 14.3 copy-start.115
  160.4 14.3 copy-start.116
  160.4 14.3 copy-start.122
  160.4 14.3 copy-start.123
  160.4 14.3 copy-start.129
  160.4 14.3 copy-start.130
  160.4 14.3 copy-start.133
  160.5 16.2 copy-start.103
  160.5 16.2 copy-start.104
  160.5 17.3 %copy-start.109 = (s32[1536]{0:T(1024)S(1)}, s32[1536]{0:T(1024)}, u32[]{:S(2)}) copy-start(s32[1536]{0:T(1024)} %get-tuple-element.218) | copy-start | bytes 18436
  160.5 17.3 %copy-start.110 = (s32[1536]{0:T(1024)S(1)}, s32[1536]{0:T(1024)}, u32[]{:S(2)}) copy-start(s32[1536]{0:T(1024)} %get-tuple-element.219) | copy-start | bytes 18436
  160.5 17.3 %copy-start.127 = (s32[1,512]{1,0:T(1,128)S(1)}, s32[1,512]{1,0:T(1,128)}, u32[]{:S(2)}) copy-start(s32[1,512]{1,0:T(1,128)} %get-tuple-element.271) | copy-start | bytes 6148
  160.5 17.3 %copy-start.128 = (s32[1,512]{1,0:T(1,128)S(1)}, s32[1,512]{1,0:T(1,128)}, u32[]{:S(2)}) copy-start(s32[1,512]{1,0:T(1,128)} %get-tuple-element.275) | copy-start | bytes 6148
  160.5 17.3 %copy-start.132 = (s32[512]{0:T(512)S(1)}, s32[512]{0:T(512)}, u32[]{:S(2)}) copy-start(s32[512]{0:T(512)} %iota_add_fusion.1) | copy-start | bytes 6148
  173.7 13.4 copy-start.111
  177.8 25.8 %copy-start.113 = (f32[1,2048]{1,0:T(1,128)S(1)}, f32[1,2048]{1,0:T(1,128)}, u32[]{:S(2)}) copy-start(f32[1,2048]{1,0:T(1,128)} %get-tuple-element.266) | copy-start | bytes 24580
  177.8 25.8 %copy-start.114 = (f32[1,2048]{1,0:T(1,128)S(1)}, f32[1,2048]{1,0:T(1,128)}, u32[]{:S(2)}) copy-start(f32[1,2048]{1,0:T(1,128)} %get-tuple-element.267) | copy-start | bytes 24580
  177.8 25.8 %copy-start.136 = (f32[8]{0:T(128)S(1)}, f32[8]{0:T(128)}, u32[]{:S(2)}) copy-start(f32[8]{0:T(128)} %multiply_power_fusion) | copy-start | bytes 100
  181.1 19.0 %all-to-all-start.1 = ((bf16[4,512,128]{1,2,0:T(8,128)(2,1)}), bf16[4,512,128]{1,2,0:T(8,128)(2,1)S(1)}, u32[]{:S(2)}, u32[]{:S(2)}) async-start(bf16[4,512,128]{1,2,0:T(8,128)(2,1)} %stack.32), calls=%async_computation.1 | async-start | bytes 1048576 | tf_op jit(solution)/shard_map/all_to_all | solution.py:207
  200.1 23.1 %all-to-all-start.6 = ((bf16[512,4,192]{0,2,1:T(8,128)(2,1)}), bf16[512,4,192]{0,2,1:T(8,128)(2,1)S(1)}, u32[]{:S(2)}, u32[]{:S(2)}) async-start(bf16[512,4,192]{0,2,1:T(8,128)(2,1)} %bitcast.61), calls=%async_computation.6 | async-start | bytes 1572864 | tf_op jit(solution)/shard_map/all_to_all | solution.py:244
  204.8 22.8 %copy-start.117 = (s32[1,512]{1,0:T(1,128)S(1)}, s32[1,512]{1,0:T(1,128)}, u32[]{:S(2)}) copy-start(s32[1,512]{1,0:T(1,128)} %get-tuple-element.270) | copy-start | bytes 6148
  204.8 22.8 %copy-start.118 = (s32[1,512]{1,0:T(1,128)S(1)}, s32[1,512]{1,0:T(1,128)}, u32[]{:S(2)}) copy-start(s32[1,512]{1,0:T(1,128)} %get-tuple-element.273) | copy-start | bytes 6148
  204.8 22.8 %copy-start.131 = (s32[512]{0:T(512)S(1)}, s32[512]{0:T(512)}, u32[]{:S(2)}) copy-start(s32[512]{0:T(512)} %iota_add_fusion.3) | copy-start | bytes 6148
  223.1 24.1 %all-to-all-start = ((bf16[512,4,192]{0,2,1:T(8,128)(2,1)}), bf16[512,4,192]{0,2,1:T(8,128)(2,1)}, u32[]{:S(2)}, u32[]{:S(2)}) async-start(bf16[512,4,192]{0,2,1:T(8,128)(2,1)} %bitcast.4), calls=%async_computation | async-start | bytes 1572864 | tf_op jit(solution)/shard_map/all_to_all | solution.py:210
  247.2 23.1 %all-to-all-start.3 = ((bf16[512,4,192]{0,2,1:T(8,128)(2,1)}), bf16[512,4,192]{0,2,1:T(8,128)(2,1)S(1)}, u32[]{:S(2)}, u32[]{:S(2)}) async-start(bf16[512,4,192]{0,2,1:T(8,128)(2,1)} %bitcast.34), calls=%async_computation.3 | async-start | bytes 1572864 | tf_op jit(solution)/shard_map/all_to_all | solution.py:210
  257.7 18.7 %copy-start.79 = (pred[512,512]{0,1:T(8,128)(4,1)S(1)}, pred[512,512]{0,1:T(8,128)(4,1)}, u32[]{:S(2)}) copy-start(pred[512,512]{0,1:T(8,128)(4,1)} %get-tuple-element.293) | copy-start | bytes 786436
  270.3 24.3 %all-to-all-start.8 = ((bf16[512,4,192]{0,2,1:T(8,128)(2,1)}), bf16[512,4,192]{0,2,1:T(8,128)(2,1)}, u32[]{:S(2)}, u32[]{:S(2)}) async-start(bf16[512,4,192]{0,2,1:T(8,128)(2,1)} %bitcast.80), calls=%async_computation.9 | async-start | bytes 1572864 | tf_op jit(solution)/shard_map/all_to_all | solution.py:244
  277.5 21.9 %copy-start.94 = (f32[512,3]{0,1:T(4,128)}, f32[512,3]{0,1:T(4,128)S(1)}, u32[]{:S(2)}) copy-start(f32[512,3]{0,1:T(4,128)S(1)} %log_add_fusion.3) | copy-start | bytes 18436
  296.6 24.8 %copy-start.40 = (bf16[1,512,192]{1,2,0:T(8,128)(2,1)}, bf16[1,512,192]{1,2,0:T(8,128)(2,1)S(1)}, u32[]{:S(2)}) copy-start(bf16[1,512,192]{1,2,0:T(8,128)(2,1)S(1)} %get-tuple-element.249) | copy-start | bytes 589828
  304.2 18.8 %copy-start.3 = (f32[512,3,1024]{2,0,1:T(8,128)}, f32[512,3,1024]{2,0,1:T(8,128)S(1)}, u32[]{:S(2)}) copy-start(f32[512,3,1024]{2,0,1:T(8,128)S(1)} %get-tuple-element.314) | copy-start | bytes 18874372
  305.7 17.3 %copy-start.92 = (f32[512,3]{0,1:T(4,128)}, f32[512,3]{0,1:T(4,128)S(1)}, u32[]{:S(2)}) copy-start(f32[512,3]{0,1:T(4,128)S(1)} %log_add_fusion.2) | copy-start | bytes 18436
  329.6 28.0 %copy-start.2 = (f32[512,3,1536]{2,0,1:T(8,128)}, f32[512,3,1536]{2,0,1:T(8,128)S(1)}, u32[]{:S(2)}) copy-start(f32[512,3,1536]{2,0,1:T(8,128)S(1)} %get-tuple-element.312) | copy-start | bytes 28311556
  366.5 57.1 %copy-start.1 = (f32[512,3,2048]{2,0,1:T(8,128)}, f32[512,3,2048]{2,0,1:T(8,128)S(1)}, u32[]{:S(2)}) copy-start(f32[512,3,2048]{2,0,1:T(8,128)S(1)} %get-tuple-element.310) | copy-start | bytes 37748740
  436.0 33.6 %all-to-all-start.5 = ((bf16[4,512,192]{1,2,0:T(8,128)(2,1)}), bf16[4,512,192]{1,2,0:T(8,128)(2,1)S(1)}, u32[]{:S(2)}, u32[]{:S(2)}) async-start(bf16[4,512,192]{1,2,0:T(8,128)(2,1)} %bitcast.514), calls=%async_computation.5 | async-start | bytes 1572864 | tf_op jit(solution)/shard_map/all_to_all | solution.py:214
  439.6 129.0 %reduce-scatter.3.cloned.1.call-start = ((), (), s32[]{:S(2)}) async-start(), calls=%async_computation.12 | async-start | bytes 1310720 | tf_op jit(solution)/shard_map/reduce_scatter | solution.py:259
  450.9 32.2 %copy-start.93 = (f32[512,3]{0,1:T(4,128)S(1)}, f32[512,3]{0,1:T(4,128)}, u32[]{:S(2)}) copy-start(f32[512,3]{0,1:T(4,128)} %copy-done.92) | copy-start | bytes 18436
  469.6 17.6 %copy-start.28 = (bf16[4,512,192]{1,2,0:T(8,128)(2,1)}, bf16[4,512,192]{1,2,0:T(8,128)(2,1)S(1)}, u32[]{:S(2)}) copy-start(bf16[4,512,192]{1,2,0:T(8,128)(2,1)S(1)} %all-to-all-done.5) | copy-start | bytes 2359300
  469.6 23.9 %all-to-all-start.2 = ((bf16[4,512,192]{1,2,0:T(8,128)(2,1)}), bf16[4,512,192]{1,2,0:T(8,128)(2,1)}, u32[]{:S(2)}, u32[]{:S(2)}) async-start(bf16[4,512,192]{1,2,0:T(8,128)(2,1)} %bitcast.562), calls=%async_computation.2 | async-start | bytes 1572864 | tf_op jit(solution)/shard_map/all_to_all | solution.py:214
  493.5 22.4 %all-to-all-start.7 = ((bf16[4,512,192]{1,2,0:T(8,128)(2,1)}), bf16[4,512,192]{1,2,0:T(8,128)(2,1)S(1)}, u32[]{:S(2)}, u32[]{:S(2)}) async-start(bf16[4,512,192]{1,2,0:T(8,128)(2,1)} %copy.108), calls=%async_computation.7 | async-start | bytes 1572864 | tf_op jit(solution)/shard_map/all_to_all | solution.py:256
  516.8 34.5 %all-to-all-start.9 = ((bf16[4,512,192]{1,2,0:T(8,128)(2,1)}), bf16[4,512,192]{1,2,0:T(8,128)(2,1)S(1)}, u32[]{:S(2)}, u32[]{:S(2)}) async-start(bf16[4,512,192]{1,2,0:T(8,128)(2,1)} %copy.113), calls=%async_computation.10 | async-start | bytes 1572864 | tf_op jit(solution)/shard_map/all_to_all | solution.py:256
  521.5 51.4 %reduce-scatter.5.cloned.1.call-start = ((), (), s32[]{:S(2)}) async-start(), calls=%async_computation.13 | async-start | bytes 1310720 | tf_op jit(solution)/shard_map/reduce_scatter | solution.py:259
  524.1 1015.0 %all-reduce.9.cloned.1.call-start = ((), (), s32[]{:S(2)}) async-start(), calls=%async_computation.15 | async-start | bytes 48041984
  528.9 22.5 %copy-start.99 = (f32[512]{0:T(512)S(1)}, f32[512]{0:T(512)}, u32[]{:S(2)}) copy-start(f32[512]{0:T(512)} %copy-done.98) | copy-start | bytes 6148
  565.4 15.5 copy-start.12
  607.4 15.7 copy-start.134
  639.8 49.6 %copy-start.107 = (f32[4,768]{1,0:T(4,128)S(1)}, f32[4,768]{1,0:T(4,128)}, u32[]{:S(2)}) copy-start(f32[4,768]{1,0:T(4,128)} %add.500) | copy-start | bytes 36868
  741.6 910.5 %all-reduce.7.cloned.1.call-start = ((), (), s32[]{:S(2)}) async-start(), calls=%async_computation.14 | async-start | bytes 12010496 | tf_op jit(solution)/shard_map/psum | solution.py:361
  (102 other events, 519.3 us)
Sparse Core Ops, SparseCore 0:
  445.7 34.2 reduce-scatter.2
  524.7 30.3 reduce-scatter.4
  741.7 797.3 all-reduce.8
  1551.9 100.1 all-reduce.6
